TPU v7x, 256 devices: a whole 4x4x8 slice. The times are simulated.
256 devices in a mesh: member: 16 (over x_lo, z), lat: 8 (over y, core), lon: 2 (over x_hi).
Axes of the slice: x: 4 (x_hi: 2, x_lo: 2; x = x_hi * 2 + x_lo), y: 4, z: 8, core: 2. Of those that a mesh axis runs over, the one named last changes fastest.
Arguments:
- state: float32 [32, 5, 2, 256, 1024], P('member', None, None, 'lat', 'lon'), may hold values from -4 to 4
- kick: float32 [32, 5, 2, 256, 1024], P('member', None, None, 'lat', 'lon'), may hold values from -3 to 3
- forcing: float32 [5, 2, 256, 1024], P(None, None, 'lat', 'lon'), may hold values from -4 to 4
- coupling: float32 [2, 5, 5], replicated, may hold values from -3 to 3
- clone_src: int32 [32], replicated, may hold values from 0 to 31, as said below
Outputs:
- advanced: float32 [32, 5, 2, 256, 1024], P('member', None, None, 'lat', 'lon')
Inputs may be any that keep to these rules, and one draw needn't show every extreme that they name: `clone_src`: entry m equals m for a member that is kept; a replaced member names a member that is kept.
All inputs are finite; a program needn't handle non-finite values.
Results may differ from a plain program's by a relative error of at most 0.00012.
Values sent between devices are 32-bit elements; how exact they have to be, the bound alone decides.
A program may use at most 128 MiB of HBM per device.

v0:
```python
import jax
import jax.numpy as jnp
from jax import lax
from jax.sharding import PartitionSpec as P

STEPS = 4


def with_halo(block, sides, width):
    for axis, dim in sides:
        count = lax.axis_size(axis)
        forward = [(i, i + 1) for i in range(count - 1)]
        forward.append((count - 1, 0))
        backward = [(target, source) for source, target in forward]
        low = lax.ppermute(
            lax.slice_in_dim(block, block.shape[dim] - width, None, axis=dim), axis, forward
        )
        high = lax.ppermute(lax.slice_in_dim(block, 0, width, axis=dim), axis, backward)
        block = jnp.concatenate([low, block, high], axis=dim)
    return block


def advance(padded, forcing_c, coupling):
    h = padded.shape[3] - 4
    w = padded.shape[4] - 4

    def part(di, dj):
        return padded[:, :, :, 2 + di : 2 + di + h, 2 + dj : 2 + dj + w]

    centre = part(0, 0)
    along_x = (8.0 * (part(0, 1) - part(0, -1)) - (part(0, 2) - part(0, -2))) / 12.0
    along_y = (8.0 * (part(1, 0) - part(-1, 0)) - (part(2, 0) - part(-2, 0))) / 12.0
    near = part(0, 1) + part(0, -1) + part(1, 0) + part(-1, 0)
    far_sum = part(0, 2) + part(0, -2) + part(2, 0) + part(-2, 0)
    laplace = (16.0 * near - far_sum - 60.0 * centre) / 12.0
    wind_u = centre[:, 0:1]
    wind_v = centre[:, 1:2]
    mixed = jnp.einsum("kvw,mwkij->mvkij", coupling, centre, precision=lax.Precision.HIGHEST)
    return centre + (
        -0.05 * (wind_u * along_x + wind_v * along_y)
        + 0.05 * laplace
        + 0.25 * mixed
        + 0.1 * forcing_c
    )


def shards(state, kick, forcing, coupling, clone_src):
    per_dev = state.shape[0]
    group = lax.axis_index("member")
    sources = lax.dynamic_slice_in_dim(clone_src, group * per_dev, per_dev)
    piece = lax.all_gather(state, "member", axis=0, tiled=True)
    count = piece.shape[0]
    inside = (sources >= 0) & (sources < count)
    rows = jnp.take(piece, jnp.clip(sources, 0, count - 1), axis=0)
    field = jnp.where(inside[:, None, None, None, None], rows, jnp.zeros_like(state))
    field = field + kick
    lat_dev = state.shape[3]
    lat_total = lat_dev * lax.axis_size("lat")
    base = lax.axis_index("lat") * lat_dev

    def zero_rows(values, first_row):
        rows = first_row + jnp.arange(values.shape[3], dtype=jnp.int32)
        keep = (rows >= 0) & (rows < lat_total)
        return jnp.where(keep[:, None], values, 0.0)

    for step in range(STEPS):
        padded = with_halo(field, (("lat", 3), ("lon", 4)), 2)
        padded = zero_rows(padded, base - 2)
        field = advance(padded, forcing, coupling)
    return field


def solution(mesh):
    in_specs = (
        P("member", None, None, "lat", "lon"),
        P("member", None, None, "lat", "lon"),
        P(None, None, "lat", "lon"),
        P(),
        P(),
    )
    out_specs = P("member", None, None, "lat", "lon")
    return jax.shard_map(shards, mesh=mesh, in_specs=in_specs, out_specs=out_specs, check_vma=False)
```

profile of v0, /device:TPU:4, one launch (start us, length us, event | category | flops | bytes accessed | tf_op | source)
XLA Modules:
  0.0 357.4 jit_solution(12120643734006682233)
XLA Ops:
  6.5 0.7 all-gather.2.cloned.1.call-update
  7.3 0.7 compare_and_fusion
  8.0 231.1 %all-gather.2.cloned.1.call-done = f32[32,5,2,32,512]{4,3,2,1,0:T(8,128)} async-done(((f32[2,5,2,32,512]{4,3,2,1,0:T(8,128)}), f32[32,5,2,32,512]{4,3,2,1,0:T(8,128)}) %all-gather.2.cloned.1.call-update) | async-done | bytes 20971536 | tf_op jit(solution)/shard_map/all_gather | solution.py:51
  239.1 7.6 %gather_fusion = f32[2,5,2,32,512]{4,3,2,1,0:T(8,128)S(1)} fusion(f32[32,5,2,32,512]{4,3,2,1,0:T(8,128)} %all-gather.2.cloned.1.call-done, s32[1024]{0:T(1024)S(1)} %pad_clamp_fusion), kind=kCustom, calls=%fused_computation | custom fusion | bytes 2621448 | tf_op jit(solution)/shard_map/jit(_take)/gather | solution.py:54
  246.7 3.9 %copy_add_fusion = f32[2,5,2,32,512]{4,1,3,0,2:T(8,128)S(1)} fusion(f32[2,5,2,32,512]{4,3,2,1,0:T(8,128)} %param.6, f32[2,5,2,32,512]{4,3,2,1,0:T(8,128)S(1)} %gather_fusion, pred[2]{0:T(512)(128)(4,1)S(1)} %get-tuple-element.5, pred[2]{0:T(512)(128)(4,1)S(1)} %get-tuple-element.31), kind=kLoop, calls=%fused_computation.17 | loop fusion | flops 983040 | bytes 3932164 | tf_op jit(solution)/shard_map/add | solution.py:56
  250.6 2.9 collective-permute-start.1
  253.6 0.1 broadcast_multiply_fusion
  253.7 2.6 collective-permute-done
  256.2 1.8 pad_maximum_fusion.11
  258.1 1.3 copy.23
  259.3 0.3 copy.24
  259.6 0.9 collective-permute-start.3
  260.5 2.7 collective-permute-start.2
  263.2 1.4 copy.28
  264.6 1.2 collective-permute-done.2
  265.8 0.4 copy.25
  266.2 0.4 copy.26
  266.5 1.9 maximum_select_fusion
  268.5 1.1 slice_multiply_fusion.7
  269.7 6.2 %fusion.7 = f32[2,5,2,32,512]{4,1,3,0,2:T(8,128)S(1)} fusion(f32[2,5,2,36,516]{4,1,3,0,2:T(8,128)S(1)} %maximum_select_fusion, f32[5,2,32,512]{3,0,2,1:T(8,128)S(1)} %copy-done.1, f32[2,2,32,512]{3,2,0,1:T(8,128)S(1)} %get-tuple-element.32, f32[2,2,32,512]{3,2,0,1:T(8,128)S(1)} %get-tuple-element.33, f32[2,5,5,1,1]{2,0,1,4,3:T(2,128)S(1)} %bitcast.50), kind=kOutput, calls=%fused_computation.16 | convolution fusion | flops 28835840 | bytes 23860224 | tf_op jit(solution)/shard_map/kvw,mwkij->mvkij/dot_general | solution.py:38
  276.0 0.0 collective-permute-start.4
  276.0 2.9 collective-permute-start.5
  279.0 2.6 collective-permute-done.4
  281.6 0.2 pad_maximum_fusion.8
  281.8 0.8 copy.29
  282.7 2.7 collective-permute-start.6
  285.4 0.3 copy.30
  285.6 1.1 collective-permute-start.7
  286.7 1.5 collective-permute-done.6
  288.2 0.4 copy.31
  288.5 2.7 collective-permute-done.7
  291.3 1.1 copy.32
  292.3 1.1 maximum_select_fusion.1
  293.4 1.1 slice_multiply_fusion.5
  294.6 6.2 %fusion.5 = f32[2,5,2,32,512]{4,1,3,0,2:T(8,128)S(1)} fusion(f32[2,5,2,36,516]{4,1,3,0,2:T(8,128)S(1)} %maximum_select_fusion.1, f32[2,2,32,512]{3,2,0,1:T(8,128)S(1)} %bitcast.58, f32[2,2,32,512]{3,2,0,1:T(8,128)S(1)} %bitcast.55, f32[5,2,32,512]{3,0,2,1:T(8,128)S(1)} %copy-done.2, f32[2,5,5,1,1]{2,0,1,4,3:T(2,128)S(1)} %bitcast.53), kind=kOutput, calls=%fused_computation.13 | convolution fusion | flops 28835840 | bytes 23860224 | tf_op jit(solution)/shard_map/kvw,mwkij->mvkij/dot_general | solution.py:38
  300.9 2.9 collective-permute-start.9
  303.9 2.6 collective-permute-done.8
  306.5 0.2 pad_maximum_fusion.5
  306.8 0.8 copy.34
  307.6 0.8 collective-permute-start.10
  308.4 0.3 copy.35
  308.7 2.8 collective-permute-start.11
  311.5 1.6 collective-permute-done.10
  313.1 0.4 copy.36
  313.5 0.7 collective-permute-done.11
  314.2 1.1 copy.37
  315.2 1.1 maximum_select_fusion.2
  316.3 1.1 slice_multiply_fusion.3
  317.5 6.2 %fusion.3 = f32[2,5,2,32,512]{4,1,3,0,2:T(8,128)S(1)} fusion(f32[2,5,2,36,516]{4,1,3,0,2:T(8,128)S(1)} %maximum_select_fusion.2, f32[2,2,32,512]{3,2,0,1:T(8,128)S(1)} %bitcast.59, f32[2,2,32,512]{3,2,0,1:T(8,128)S(1)} %bitcast.56, f32[5,2,32,512]{3,0,2,1:T(8,128)S(1)} %copy-done.3, f32[2,5,5,1,1]{2,0,1,4,3:T(2,128)S(1)} %bitcast.52), kind=kOutput, calls=%fused_computation.10 | convolution fusion | flops 28835840 | bytes 23860224 | tf_op jit(solution)/shard_map/kvw,mwkij->mvkij/dot_general | solution.py:38
  323.8 2.9 collective-permute-start.13
  326.8 2.6 collective-permute-done.12
  329.4 0.2 pad_maximum_fusion.2
  329.7 0.8 copy.39
  330.5 2.7 collective-permute-start.14
  333.2 0.3 copy.40
  333.4 1.1 collective-permute-start.15
  334.6 1.4 collective-permute-done.14
  336.0 0.4 copy.41
  336.4 2.8 collective-permute-done.15
  339.1 1.1 copy.42
  340.2 1.1 maximum_select_fusion.3
  341.3 1.1 slice_multiply_fusion.1
  342.5 6.2 %fusion.1 = f32[2,5,2,32,512]{4,1,3,0,2:T(8,128)S(1)} fusion(f32[2,5,2,36,516]{4,1,3,0,2:T(8,128)S(1)} %maximum_select_fusion.3, f32[2,2,32,512]{3,2,0,1:T(8,128)S(1)} %bitcast.57, f32[2,2,32,512]{3,2,0,1:T(8,128)S(1)} %bitcast.54, f32[5,2,32,512]{3,0,2,1:T(8,128)S(1)} %copy-done.4, f32[2,5,5,1,1]{2,0,1,4,3:T(2,128)S(1)} %bitcast.51), kind=kOutput, calls=%fused_computation.7 | convolution fusion | flops 28835840 | bytes 23860224 | tf_op jit(solution)/shard_map/kvw,mwkij->mvkij/dot_general | solution.py:38
  348.7 1.8 copy.44
  (34 shorter events, 0.4 us)
Async XLA Ops:
  6.5 263.2 %copy-start = (f32[2,5,5]{2,0,1:T(2,128)S(1)}, f32[2,5,5]{2,0,1:T(2,128)}, u32[]{:S(2)}) copy-start(f32[2,5,5]{2,0,1:T(2,128)} %param.8) | copy-start | bytes 604
  6.5 232.6 %all-gather.2.cloned.1.call-start = ((), (), s32[]{:S(2)}) async-start(), calls=%async_computation | async-start | bytes 22282240 | tf_op jit(solution)/shard_map/all_gather | solution.py:51
  246.7 6.9 %copy-start.5 = (f32[5,2,32,512]{3,2,1,0:T(8,128)S(1)}, f32[5,2,32,512]{3,2,1,0:T(8,128)}, u32[]{:S(2)}) copy-start(f32[5,2,32,512]{3,2,1,0:T(8,128)} %param.7) | copy-start | bytes 1966084
  250.6 5.6 %collective-permute-start = (f32[2,5,2,2,512]{4,1,3,0,2:T(8,128)S(1)}, f32[2,5,2,2,512]{4,1,3,0,2:T(8,128)S(1)}, u32[]{:S(2)}, u32[]{:S(2)}) collective-permute-start(f32[2,5,2,2,512]{4,1,3,0,2:T(8,128)S(1)} %get-tuple-element.29), channel_id=1, source_target_pairs={{0,2},{2,4},{4,6},{6,8},{8,10},{10,12},{12,14},{14,0},{1,3},{3,5},... | collective-permute-start | bytes 245768 | tf_op jit(solution)/shard_map/ppermute | solution.py:15
  250.6 5.6 %collective-permute-start.1 = (f32[2,5,2,2,512]{4,1,3,0,2:T(8,128)S(1)}, f32[2,5,2,2,512]{4,1,3,0,2:T(8,128)}, u32[]{:S(2)}, u32[]{:S(2)}) collective-permute-start(f32[2,5,2,2,512]{4,1,3,0,2:T(8,128)S(1)} %get-tuple-element.30), channel_id=1, source_target_pairs={{2,0},{4,2},{6,4},{8,6},{10,8},{12,10},{14,12},{0,14},{3,1},{5,3},... | collective-permute-start | bytes 245768 | tf_op jit(solution)/shard_map/ppermute | solution.py:18
  259.6 6.6 %collective-permute-start.3 = (f32[2,5,2,36,2]{3,4,2,1,0:T(2,128)S(1)}, f32[2,5,2,36,2]{3,4,2,1,0:T(2,128)S(1)}, u32[]{:S(2)}, u32[]{:S(2)}) collective-permute-start(f32[2,5,2,36,2]{3,4,2,1,0:T(2,128)S(1)} %copy.24), channel_id=1, source_target_pairs={{1,0},{0,1},{3,2},{2,3},{5,4},{4,5},{7,6},{6,7},{9,8},{8,9},{11,10... | collective-permute-start | bytes 17288 | tf_op jit(solution)/shard_map/ppermute | solution.py:18
  260.5 5.3 %collective-permute-start.2 = (f32[2,5,2,36,2]{3,4,2,1,0:T(2,128)S(1)}, f32[2,5,2,36,2]{3,4,2,1,0:T(2,128)S(1)}, u32[]{:S(2)}, u32[]{:S(2)}) collective-permute-start(f32[2,5,2,36,2]{3,4,2,1,0:T(2,128)S(1)} %copy.23), channel_id=1, source_target_pairs={{0,1},{1,0},{2,3},{3,2},{4,5},{5,4},{6,7},{7,6},{8,9},{9,8},{10,11... | collective-permute-start | bytes 17288 | tf_op jit(solution)/shard_map/ppermute | solution.py:15
  268.5 1.2 copy-start.1
  276.0 5.6 %collective-permute-start.4 = (f32[2,5,2,2,512]{4,1,3,0,2:T(8,128)S(1)}, f32[2,5,2,2,512]{4,1,3,0,2:T(8,128)S(1)}, u32[]{:S(2)}, u32[]{:S(2)}) collective-permute-start(f32[2,5,2,2,512]{4,1,3,0,2:T(8,128)S(1)} %get-tuple-element.27), channel_id=1, source_target_pairs={{0,2},{2,4},{4,6},{6,8},{8,10},{10,12},{12,14},{14,0},{1,3},{3,5},... | collective-permute-start | bytes 245768 | tf_op jit(solution)/shard_map/ppermute | solution.py:15
  276.0 5.6 %collective-permute-start.5 = (f32[2,5,2,2,512]{4,1,3,0,2:T(8,128)S(1)}, f32[2,5,2,2,512]{4,1,3,0,2:T(8,128)S(1)}, u32[]{:S(2)}, u32[]{:S(2)}) collective-permute-start(f32[2,5,2,2,512]{4,1,3,0,2:T(8,128)S(1)} %get-tuple-element.28), channel_id=1, source_target_pairs={{2,0},{4,2},{6,4},{8,6},{10,8},{12,10},{14,12},{0,14},{3,1},{5,3},... | collective-permute-start | bytes 245768 | tf_op jit(solution)/shard_map/ppermute | solution.py:18
  282.7 5.5 %collective-permute-start.6 = (f32[2,5,2,36,2]{3,4,2,1,0:T(2,128)}, f32[2,5,2,36,2]{3,4,2,1,0:T(2,128)S(1)}, u32[]{:S(2)}, u32[]{:S(2)}) collective-permute-start(f32[2,5,2,36,2]{3,4,2,1,0:T(2,128)} %copy.29), channel_id=1, source_target_pairs={{0,1},{1,0},{2,3},{3,2},{4,5},{5,4},{6,7},{7,6},{8,9},{9,8},{10,11... | collective-permute-start | bytes 17288 | tf_op jit(solution)/shard_map/ppermute | solution.py:15
  285.6 5.7 %collective-permute-start.7 = (f32[2,5,2,36,2]{3,4,2,1,0:T(2,128)S(1)}, f32[2,5,2,36,2]{3,4,2,1,0:T(2,128)}, u32[]{:S(2)}, u32[]{:S(2)}) collective-permute-start(f32[2,5,2,36,2]{3,4,2,1,0:T(2,128)S(1)} %copy.30), channel_id=1, source_target_pairs={{1,0},{0,1},{3,2},{2,3},{5,4},{4,5},{7,6},{6,7},{9,8},{8,9},{11,10... | collective-permute-start | bytes 17288 | tf_op jit(solution)/shard_map/ppermute | solution.py:18
  293.4 1.2 copy-start.2
  300.9 5.6 %collective-permute-start.8 = (f32[2,5,2,2,512]{4,1,3,0,2:T(8,128)S(1)}, f32[2,5,2,2,512]{4,1,3,0,2:T(8,128)S(1)}, u32[]{:S(2)}, u32[]{:S(2)}) collective-permute-start(f32[2,5,2,2,512]{4,1,3,0,2:T(8,128)S(1)} %get-tuple-element.25), channel_id=1, source_target_pairs={{0,2},{2,4},{4,6},{6,8},{8,10},{10,12},{12,14},{14,0},{1,3},{3,5},... | collective-permute-start | bytes 245768 | tf_op jit(solution)/shard_map/ppermute | solution.py:15
  300.9 5.6 %collective-permute-start.9 = (f32[2,5,2,2,512]{4,1,3,0,2:T(8,128)S(1)}, f32[2,5,2,2,512]{4,1,3,0,2:T(8,128)S(1)}, u32[]{:S(2)}, u32[]{:S(2)}) collective-permute-start(f32[2,5,2,2,512]{4,1,3,0,2:T(8,128)S(1)} %get-tuple-element.26), channel_id=1, source_target_pairs={{2,0},{4,2},{6,4},{8,6},{10,8},{12,10},{14,12},{0,14},{3,1},{5,3},... | collective-permute-start | bytes 245768 | tf_op jit(solution)/shard_map/ppermute | solution.py:18
  307.6 5.5 %collective-permute-start.10 = (f32[2,5,2,36,2]{3,4,2,1,0:T(2,128)}, f32[2,5,2,36,2]{3,4,2,1,0:T(2,128)S(1)}, u32[]{:S(2)}, u32[]{:S(2)}) collective-permute-start(f32[2,5,2,36,2]{3,4,2,1,0:T(2,128)} %copy.34), channel_id=1, source_target_pairs={{0,1},{1,0},{2,3},{3,2},{4,5},{5,4},{6,7},{7,6},{8,9},{9,8},{10,11... | collective-permute-start | bytes 17288 | tf_op jit(solution)/shard_map/ppermute | solution.py:15
  308.7 5.5 %collective-permute-start.11 = (f32[2,5,2,36,2]{3,4,2,1,0:T(2,128)S(1)}, f32[2,5,2,36,2]{3,4,2,1,0:T(2,128)}, u32[]{:S(2)}, u32[]{:S(2)}) collective-permute-start(f32[2,5,2,36,2]{3,4,2,1,0:T(2,128)S(1)} %copy.35), channel_id=1, source_target_pairs={{1,0},{0,1},{3,2},{2,3},{5,4},{4,5},{7,6},{6,7},{9,8},{8,9},{11,10... | collective-permute-start | bytes 17288 | tf_op jit(solution)/shard_map/ppermute | solution.py:18
  316.3 1.2 copy-start.3
  323.8 5.6 %collective-permute-start.12 = (f32[2,5,2,2,512]{4,1,3,0,2:T(8,128)S(1)}, f32[2,5,2,2,512]{4,1,3,0,2:T(8,128)S(1)}, u32[]{:S(2)}, u32[]{:S(2)}) collective-permute-start(f32[2,5,2,2,512]{4,1,3,0,2:T(8,128)S(1)} %get-tuple-element.23), channel_id=1, source_target_pairs={{0,2},{2,4},{4,6},{6,8},{8,10},{10,12},{12,14},{14,0},{1,3},{3,5},... | collective-permute-start | bytes 245768 | tf_op jit(solution)/shard_map/ppermute | solution.py:15
  323.8 5.6 %collective-permute-start.13 = (f32[2,5,2,2,512]{4,1,3,0,2:T(8,128)S(1)}, f32[2,5,2,2,512]{4,1,3,0,2:T(8,128)S(1)}, u32[]{:S(2)}, u32[]{:S(2)}) collective-permute-start(f32[2,5,2,2,512]{4,1,3,0,2:T(8,128)S(1)} %get-tuple-element.24), channel_id=1, source_target_pairs={{2,0},{4,2},{6,4},{8,6},{10,8},{12,10},{14,12},{0,14},{3,1},{5,3},... | collective-permute-start | bytes 245768 | tf_op jit(solution)/shard_map/ppermute | solution.py:18
  330.5 5.5 %collective-permute-start.14 = (f32[2,5,2,36,2]{3,4,2,1,0:T(2,128)}, f32[2,5,2,36,2]{3,4,2,1,0:T(2,128)S(1)}, u32[]{:S(2)}, u32[]{:S(2)}) collective-permute-start(f32[2,5,2,36,2]{3,4,2,1,0:T(2,128)} %copy.39), channel_id=1, source_target_pairs={{0,1},{1,0},{2,3},{3,2},{4,5},{5,4},{6,7},{7,6},{8,9},{9,8},{10,11... | collective-permute-start | bytes 17288 | tf_op jit(solution)/shard_map/ppermute | solution.py:15
  333.4 5.7 %collective-permute-start.15 = (f32[2,5,2,36,2]{3,4,2,1,0:T(2,128)S(1)}, f32[2,5,2,36,2]{3,4,2,1,0:T(2,128)}, u32[]{:S(2)}, u32[]{:S(2)}) collective-permute-start(f32[2,5,2,36,2]{3,4,2,1,0:T(2,128)S(1)} %copy.40), channel_id=1, source_target_pairs={{1,0},{0,1},{3,2},{2,3},{5,4},{4,5},{7,6},{6,7},{9,8},{8,9},{11,10... | collective-permute-start | bytes 17288 | tf_op jit(solution)/shard_map/ppermute | solution.py:18
  341.3 1.2 copy-start.4
Sparse Core Ops, SparseCore 0:
  9.1 229.9 all-gather.1
where the time goes:
time: 358 us; the launch traced here: 357 us
  waiting for transfers between devices  254 us (71%)
  starting transfers between devices  26.7 us (7%)
  matrix products  24.9 us (7%)
  local copies, waits for them, and re-layouts  20.8 us (6%)
  other arithmetic  16.9 us (5%)
  between operations  13.8 us (4%)
    all_gather x1, waiting for transfers between devices, shards(): piece = lax.all_gather(state, 'member', axis=0, tiled=True)  231 us
    dot_general x4, matrix products, advance(): jnp.einsum('kvw,mwkij->mvkij', coupling, centre, precision=lax.Precision....  24.9 us
    ppermute x8, starting transfers between devices, with_halo(): lax.ppermute(lax.slice_in_dim(block, 0, width, axis=dim), axis, backward)  17.7 us
    ppermute x8, waiting for transfers between devices, with_halo(): lax.ppermute(lax.slice_in_dim(block, block.shape[dim] - width, None, axis...  16.2 us
    ppermute x8, starting transfers between devices, with_halo(): lax.ppermute(lax.slice_in_dim(block, block.shape[dim] - width, None, axis...  8.97 us
    gather x1, local copies, waits for them, and re-layouts, shards(): rows = jnp.take(piece, jnp.clip(sources, 0, count - 1), axis=0)  7.59 us
  transfers between devices with their start and end apart: 17, of which 12 were waited for; matrix products, arithmetic and copies ran while one was open for 1% of the time, Pallas kernels for 0%

commit v1 on v0

--- a/solution.py
+++ b/solution.py
@@ -48,7 +48,9 @@
     per_dev = state.shape[0]
     group = lax.axis_index("member")
     sources = lax.dynamic_slice_in_dim(clone_src, group * per_dev, per_dev)
-    piece = lax.all_gather(state, "member", axis=0, tiled=True)
+    piece = jnp.concatenate(
+        lax.all_to_all(jnp.stack([state] * lax.axis_size("member")), "member", 0, 0), axis=0
+    )
     count = piece.shape[0]
     inside = (sources >= 0) & (sources < count)
     rows = jnp.take(piece, jnp.clip(sources, 0, count - 1), axis=0)

time: 358 us -> 623 us (1.74)
  the two profiles are of different devices: /device:TPU:4 before, /device:TPU:162 now
where the time goes in v1:
time: 623 us; the launch traced here: 622 us
  waiting for transfers between devices  523 us (84%)
  local copies, waits for them, and re-layouts  31.9 us (5%)
  starting transfers between devices  26 us (4%)
  matrix products  24.9 us (4%)
  other arithmetic  16.2 us (3%)
    all_to_all x1, waiting for transfers between devices, shards(): lax.all_to_all(jnp.stack([state] * lax.axis_size('member')), 'member', 0, 0)  490 us
    dot_general x4, matrix products, advance(): jnp.einsum('kvw,mwkij->mvkij', coupling, centre, precision=lax.Precision....  24.9 us
    ppermute x8, waiting for transfers between devices, with_halo(): lax.ppermute(lax.slice_in_dim(block, block.shape[dim] - width, None, axis...  19.5 us
    ppermute x8, waiting for transfers between devices, with_halo(): lax.ppermute(lax.slice_in_dim(block, 0, width, axis=dim), axis, backward)  13 us
  transfers between devices with their start and end apart: 17, of which 17 were waited for; matrix products, arithmetic and copies ran while one was open for 1% of the time, Pallas kernels for 0%

profile of v1, /device:TPU:162, one launch (start us, length us, event | category | flops | bytes accessed | tf_op | source)
XLA Modules:
  0.0 622.1 jit_solution(8952431628556276216)
XLA Ops:
  0.0 11.0 %stack.2 = f32[16,2,5,2,32,512]{5,4,3,2,1,0:T(8,128)} broadcast(f32[2,5,2,32,512]{4,3,2,1,0:T(8,128)} %param.5), dimensions={1,2,3,4,5} | broadcast | bytes 22282240 | tf_op jit(solution)/shard_map/stack | solution.py:52
  11.0 7.8 %all-to-all-start = ((f32[16,2,5,2,32,512]{5,4,3,2,1,0:T(8,128)}), f32[16,2,5,2,32,512]{5,4,3,2,1,0:T(8,128)}, u32[]{:S(2)}, u32[]{:S(2)}) async-start(f32[16,2,5,2,32,512]{5,4,3,2,1,0:T(8,128)} %stack.2), calls=%async_computation | async-start | bytes 41943040 | tf_op jit(solution)/shard_map/all_to_all | solution.py:52
  18.9 490.1 %all-to-all-done = f32[16,2,5,2,32,512]{5,4,3,2,1,0:T(8,128)} async-done(((f32[16,2,5,2,32,512]{5,4,3,2,1,0:T(8,128)}), f32[16,2,5,2,32,512]{5,4,3,2,1,0:T(8,128)}, u32[]{:S(2)}, u32[]{:S(2)}) %all-to-all-start) | async-done | bytes 20971552 | tf_op jit(solution)/shard_map/all_to_all | solution.py:52
  509.0 7.6 %gather_fusion = f32[2,5,2,32,512]{4,3,2,1,0:T(8,128)S(1)} fusion(f32[32,5,2,32,512]{4,3,2,1,0:T(8,128)} %bitcast, s32[1024]{0:T(1024)S(1)} %pad_clamp_fusion), kind=kCustom, calls=%fused_computation | custom fusion | bytes 2621448 | tf_op jit(solution)/shard_map/jit(_take)/gather | solution.py:56
  516.6 3.9 copy_add_fusion
  520.5 1.8 collective-permute-start.1
  522.4 2.4 collective-permute-done.1
  524.8 3.2 collective-permute-done
  528.0 1.8 pad_maximum_fusion.11
  529.8 1.3 copy.24
  531.1 2.2 collective-permute-start.3
  533.3 0.3 copy.23
  533.6 1.5 collective-permute-start.2
  535.0 1.4 copy.28
  536.5 0.4 copy.26
  536.8 2.1 collective-permute-done.2
  538.9 0.4 copy.25
  539.3 1.9 maximum_select_fusion
  541.2 1.1 slice_multiply_fusion.7
  542.5 6.2 %fusion.7 = f32[2,5,2,32,512]{4,1,3,0,2:T(8,128)S(1)} fusion(f32[2,5,2,36,516]{4,1,3,0,2:T(8,128)S(1)} %maximum_select_fusion, f32[5,2,32,512]{3,0,2,1:T(8,128)S(1)} %copy-done.1, f32[2,2,32,512]{3,2,0,1:T(8,128)S(1)} %get-tuple-element.32, f32[2,2,32,512]{3,2,0,1:T(8,128)S(1)} %get-tuple-element.33, f32[2,5,5,1,1]{2,0,1,4,3:T(2,128)S(1)} %bitcast.51), kind=kOutput, calls=%fused_computation.16 | convolution fusion | flops 28835840 | bytes 23860224 | tf_op jit(solution)/shard_map/kvw,mwkij->mvkij/dot_general | solution.py:38
  548.8 0.5 collective-permute-start.4
  549.3 2.0 collective-permute-done.5
  551.3 3.1 collective-permute-done.4
  554.6 0.8 copy.30
  555.4 1.4 collective-permute-start.7
  556.8 0.3 copy.29
  557.1 2.4 collective-permute-start.6
  559.5 1.5 collective-permute-done.7
  560.9 0.4 copy.32
  561.3 1.5 collective-permute-done.6
  562.7 1.1 copy.31
  563.8 1.1 maximum_select_fusion.1
  564.9 1.1 slice_multiply_fusion.5
  566.1 6.2 %fusion.5 = f32[2,5,2,32,512]{4,1,3,0,2:T(8,128)S(1)} fusion(f32[2,5,2,36,516]{4,1,3,0,2:T(8,128)S(1)} %maximum_select_fusion.1, f32[2,2,32,512]{3,2,0,1:T(8,128)S(1)} %bitcast.56, f32[2,2,32,512]{3,2,0,1:T(8,128)S(1)} %bitcast.59, f32[5,2,32,512]{3,0,2,1:T(8,128)S(1)} %copy-done.2, f32[2,5,5,1,1]{2,0,1,4,3:T(2,128)S(1)} %bitcast.54), kind=kOutput, calls=%fused_computation.13 | convolution fusion | flops 28835840 | bytes 23860224 | tf_op jit(solution)/shard_map/kvw,mwkij->mvkij/dot_general | solution.py:38
  572.4 0.5 collective-permute-start.8
  572.9 2.0 collective-permute-done.9
  574.9 3.1 collective-permute-done.8
  578.0 0.2 pad_maximum_fusion.5
  578.3 0.8 copy.35
  579.1 2.1 collective-permute-start.11
  581.2 0.3 copy.34
  581.5 1.5 collective-permute-start.10
  583.0 1.6 collective-permute-done.11
  584.6 0.4 copy.37
  585.0 2.0 collective-permute-done.10
  587.0 1.1 copy.36
  588.0 1.1 maximum_select_fusion.2
  589.1 1.1 slice_multiply_fusion.3
  590.3 6.2 %fusion.3 = f32[2,5,2,32,512]{4,1,3,0,2:T(8,128)S(1)} fusion(f32[2,5,2,36,516]{4,1,3,0,2:T(8,128)S(1)} %maximum_select_fusion.2, f32[2,2,32,512]{3,2,0,1:T(8,128)S(1)} %bitcast.57, f32[2,2,32,512]{3,2,0,1:T(8,128)S(1)} %bitcast.60, f32[5,2,32,512]{3,0,2,1:T(8,128)S(1)} %copy-done.3, f32[2,5,5,1,1]{2,0,1,4,3:T(2,128)S(1)} %bitcast.53), kind=kOutput, calls=%fused_computation.10 | convolution fusion | flops 28835840 | bytes 23860224 | tf_op jit(solution)/shard_map/kvw,mwkij->mvkij/dot_general | solution.py:38
  596.6 0.5 collective-permute-start.12
  597.1 2.0 collective-permute-done.13
  599.1 3.1 collective-permute-done.12
  602.5 0.8 copy.40
  603.3 1.4 collective-permute-start.15
  604.7 0.3 copy.39
  605.0 2.4 collective-permute-start.14
  607.4 1.4 collective-permute-done.15
  608.8 0.4 copy.42
  609.2 1.5 collective-permute-done.14
  610.7 1.1 copy.41
  611.7 1.1 maximum_select_fusion.3
  612.8 1.1 slice_multiply_fusion.1
  614.0 6.2 fusion.1
  620.2 1.8 copy.44
  (36 shorter events, 1.0 us)
Async XLA Ops:
  0.0 542.4 %copy-start = (f32[2,5,5]{2,0,1:T(2,128)S(1)}, f32[2,5,5]{2,0,1:T(2,128)}, u32[]{:S(2)}) copy-start(f32[2,5,5]{2,0,1:T(2,128)} %param.8) | copy-start | bytes 604
  11.0 7.8 %copy-start.6 = (s32[32]{0:T(128)S(1)}, s32[32]{0:T(128)}, u32[]{:S(2)}) copy-start(s32[32]{0:T(128)} %param.9) | copy-start | bytes 388
  11.0 498.0 %all-to-all-start = ((f32[16,2,5,2,32,512]{5,4,3,2,1,0:T(8,128)}), f32[16,2,5,2,32,512]{5,4,3,2,1,0:T(8,128)}, u32[]{:S(2)}, u32[]{:S(2)}) async-start(f32[16,2,5,2,32,512]{5,4,3,2,1,0:T(8,128)} %stack.2), calls=%async_computation | async-start | bytes 41943040 | tf_op jit(solution)/shard_map/all_to_all | solution.py:52
  516.6 5.7 copy-start.5
  520.5 4.3 collective-permute-start.1
  522.3 5.7 collective-permute-start
  531.1 5.4 collective-permute-start.3
  533.6 5.4 collective-permute-start.2
  541.2 1.2 copy-start.1
  548.7 2.5 collective-permute-start.5
  548.8 5.6 collective-permute-start.4
  555.4 5.5 collective-permute-start.7
  557.1 5.7 collective-permute-start.6
  564.9 1.2 copy-start.2
  572.4 2.5 collective-permute-start.9
  572.4 5.6 collective-permute-start.8
  579.1 5.5 collective-permute-start.11
  581.5 5.5 collective-permute-start.10
  589.1 1.2 copy-start.3
  596.6 2.5 collective-permute-start.13
  596.6 5.6 collective-permute-start.12
  603.3 5.5 collective-permute-start.15
  605.0 5.7 collective-permute-start.14
  612.8 1.2 copy-start.4
